TPU v7x, 256 devices: a whole 4x4x8 slice. The times are simulated.
256 devices in a mesh: dp: 4 (over y), mp: 64 (over x, z, core).
Axes of the slice: x: 4, y: 4, z: 8, core: 2. Of those that a mesh axis runs over, the one named last changes fastest.
Arguments:
- inputs: bfloat16 [8, 256, 6144], P('dp', None, 'mp'), may hold values from -6 to 6
- cotangent: bfloat16 [8, 256, 6144], P('dp', None, 'mp'), may hold values from -6 to 6
- w_up: bfloat16 [6144, 24576], P('dp', 'mp'), may hold values from -0.078125 to 0.078125
- w_down: bfloat16 [24576, 6144], P('mp', 'dp'), may hold values from -0.0390625 to 0.0390625
- thresholds: float32 [2], replicated, may hold values from 23592.96 to 58982.4
Outputs:
- grad_up: float32 [6144, 24576], P('dp', 'mp')
- grad_down: float32 [24576, 6144], P('mp', 'dp')
- norms: float32 [8, 2], P('dp')
All inputs are finite; a program needn't handle non-finite values.
Results may differ from a plain program's by a relative error of at most 0.0085.
Values may be sent and summed in bfloat16 or wider, within the bound.
A program may use at most 128 MiB of HBM per device.

v0:
```python
import jax
import jax.numpy as jnp
from jax import lax
from jax.sharding import PartitionSpec as P

inv_root_two = 0.7071067811865476
inv_root_two_pi = 0.3989422804014327


def sent_to_all(shard, axis):
    copies = jnp.broadcast_to(shard, (lax.axis_size(axis), *shard.shape))
    return lax.all_to_all(copies, axis, split_axis=0, concat_axis=0, tiled=True)


def taken_together(shard, axis):
    return sent_to_all(shard, axis).sum(axis=0)


def packed_total(arrays, axis):
    line, at, outs = (jnp.concatenate([a.reshape(-1) for a in arrays]), 0, [])
    running = taken_together(line, axis)
    for a in arrays:
        outs.append(running[at : at + a.size].reshape(a.shape))
        at += a.size
    return tuple(outs)


def split_up(shard, dim, count):
    shape = shard.shape
    pieces = shard.reshape(*shape[:dim], count, shape[dim] // count, *shape[dim + 1 :])
    return jnp.moveaxis(pieces, dim, 0)


def sum_at_owner(shard, axis, dim):
    pieces = split_up(shard, dim, lax.axis_size(axis))
    arrived = lax.all_to_all(pieces, axis, split_axis=0, concat_axis=0, tiled=True)
    return arrived.astype(jnp.float32).sum(axis=0)


def normal_cdf(value):
    return 0.5 * (1.0 + lax.erf(value * inv_root_two))


def gram_of(array, images, patches):
    cube = array.reshape(images, patches, -1)
    return jnp.einsum("btd,bsd->bts", cube, cube, preferred_element_type=jnp.float32)


def on_device(inputs, cotangent, w_up, w_down, thresholds):
    images, patches, local_feats = inputs.shape
    count_rows = images * patches
    x_whole = lax.all_gather(inputs, "mp", axis=2, tiled=True).reshape(count_rows, -1)
    hidden_local = w_up.shape[1]
    columns = x_whole
    pre = jnp.dot(
        columns, lax.all_gather(w_up, "dp", axis=0, tiled=True), preferred_element_type=jnp.float32
    )
    act = (pre * normal_cdf(pre)).astype(jnp.bfloat16)
    dy_whole = lax.all_gather(cotangent, "mp", axis=2, tiled=True).reshape(count_rows, -1)
    columns = dy_whole
    dact = lax.dot_general(
        columns,
        lax.all_gather(w_down, "dp", axis=1, tiled=True),
        (((1,), (1,)), ((), ())),
        preferred_element_type=jnp.float32,
    )
    slope = normal_cdf(pre) + pre * jnp.exp(-0.5 * pre * pre) * inv_root_two_pi
    dpre = (dact * slope).astype(jnp.bfloat16)
    gram_dpre = gram_of(dpre, images, patches)
    gram_act = gram_of(act, images, patches)
    part_up = jnp.sum(gram_of(x_whole, images, patches) * gram_dpre, axis=(1, 2))
    part_down = jnp.sum(gram_act * gram_of(dy_whole, images, patches), axis=(1, 2))
    sq_up, sq_down = packed_total((part_up, part_down), "mp")
    norms = jnp.stack([jnp.sqrt(sq_up), jnp.sqrt(sq_down)], axis=1)
    factor = jnp.minimum(1.0, thresholds[None, :] / (norms + 1e-06))
    dpre_clip = (
        (
            factor[:, 0][:, None, None]
            * dpre.reshape(images, patches, hidden_local).astype(jnp.float32)
        )
        .astype(jnp.bfloat16)
        .reshape(count_rows, hidden_local)
    )
    cot_clip = (
        (factor[:, 1][:, None, None] * dy_whole.reshape(images, patches, -1).astype(jnp.float32))
        .astype(jnp.bfloat16)
        .reshape(count_rows, -1)
    )
    columns = x_whole
    grad_up = lax.psum_scatter(
        lax.dot_general(
            columns, dpre_clip, (((0,), (0,)), ((), ())), preferred_element_type=jnp.float32
        ).astype(jnp.bfloat16),
        "dp",
        scatter_dimension=0,
        tiled=True,
    ).astype(jnp.float32)
    down_full = lax.dot_general(
        act, cot_clip, (((0,), (0,)), ((), ())), preferred_element_type=jnp.float32
    )
    grad_down = sum_at_owner(down_full.astype(jnp.bfloat16), "dp", 1)
    return (grad_up, grad_down, norms)


def solution(mesh):
    in_specs = (P("dp", None, "mp"), P("dp", None, "mp"), P("dp", "mp"), P("mp", "dp"), P())
    out_specs = (P("dp", "mp"), P("mp", "dp"), P("dp", None))
    return jax.shard_map(
        on_device, mesh=mesh, in_specs=in_specs, out_specs=out_specs, check_vma=False
    )
```

profile of v0, /device:TPU:1, one launch (start us, length us, event | category | flops | bytes accessed | tf_op | source)
XLA Modules:
  0.0 445.1 jit_solution(11769768210793305239)
XLA Ops:
  7.2 0.0 all-gather.5.cloned.1.call-start
  7.2 0.7 all-gather.5.cloned.1.call-update
  7.9 0.0 all-gather.7.cloned.1.call-start
  7.9 0.7 all-gather.7.cloned.1.call-update
  8.6 0.0 all-gather.11.cloned.1.call-start
  8.7 0.7 all-gather.11.cloned.1.call-update
  9.4 0.0 all-gather.9.cloned.1.call-start
  9.4 0.5 all-gather.9.cloned.1.call-update
  10.0 85.6 %all-gather.5.cloned.1.call-done = bf16[2,256,6144]{1,2,0:T(8,128)(2,1)} async-done(((bf16[2,256,96]{1,2,0:T(8,128)(2,1)}), bf16[2,256,6144]{1,2,0:T(8,128)(2,1)}) %all-gather.5.cloned.1.call-update) | async-done | bytes 6291472 | tf_op jit(solution)/shard_map/all_gather | solution.py:52
  95.5 8.7 %copy.32 = bf16[2,256,6144]{2,1,0:T(8,128)(2,1)} copy(bf16[2,256,6144]{1,2,0:T(8,128)(2,1)} %all-gather.5.cloned.1.call-done) | data formatting | bytes 12582912 | tf_op jit(solution)/shard_map/all_gather | solution.py:52
  104.2 71.4 %all-gather.7.cloned.1.call-done = bf16[2,256,6144]{1,2,0:T(8,128)(2,1)} async-done(((bf16[2,256,96]{1,2,0:T(8,128)(2,1)}), bf16[2,256,6144]{1,2,0:T(8,128)(2,1)}) %all-gather.7.cloned.1.call-update) | async-done | bytes 6291472 | tf_op jit(solution)/shard_map/all_gather | solution.py:59
  175.6 8.7 %copy.31 = bf16[2,256,6144]{2,1,0:T(8,128)(2,1)} copy(bf16[2,256,6144]{1,2,0:T(8,128)(2,1)} %all-gather.7.cloned.1.call-done) | data formatting | bytes 12582912 | tf_op jit(solution)/shard_map/all_gather | solution.py:59
  184.3 44.5 %all-gather.11.cloned.1.call-done = bf16[6144,384]{1,0:T(8,128)(2,1)} async-done(((bf16[1536,384]{1,0:T(8,128)(2,1)}), bf16[6144,384]{1,0:T(8,128)(2,1)}) %all-gather.11.cloned.1.call-update) | async-done | bytes 4718608 | tf_op jit(solution)/shard_map/all_gather | solution.py:56
  228.8 7.0 %multiply_convert_fusion.2 = (bf16[512,384]{1,0:T(8,128)(2,1)S(1)}, f32[512,384]{1,0:T(8,128)S(1)}) fusion(bf16[512,6144]{1,0:T(8,128)(2,1)} %bitcast.47, bf16[6144,384]{1,0:T(8,128)(2,1)} %all-gather.11.cloned.1.call-done), kind=kOutput, calls=%fused_computation.18 | convolution fusion | flops 2416902144 | bytes 12189696 | tf_op jit(solution)/shard_map/dot_general | solution.py:55
  235.7 50.3 %all-gather.9.cloned.1.call-done = bf16[384,6144]{1,0:T(8,128)(2,1)} async-done(((bf16[384,1536]{1,0:T(8,128)(2,1)}), bf16[384,6144]{1,0:T(8,128)(2,1)}) %all-gather.9.cloned.1.call-update) | async-done | bytes 4718608 | tf_op jit(solution)/shard_map/all_gather | solution.py:63
  286.0 7.7 %fusion.1 = bf16[512,384]{1,0:T(8,128)(2,1)S(1)} fusion(bf16[512,6144]{1,0:T(8,128)(2,1)} %bitcast.46, bf16[384,6144]{1,0:T(8,128)(2,1)} %all-gather.9.cloned.1.call-done, f32[512,384]{1,0:T(8,128)S(1)} %get-tuple-element.25), kind=kOutput, calls=%fused_computation.7 | convolution fusion | flops 2417885184 | bytes 12189696 | tf_op jit(solution)/shard_map/dot_general | solution.py:61
  293.7 0.3 fusion.9
  294.0 0.0 slice-start
  294.0 0.3 fusion.10
  294.4 0.0 slice-start.1
  294.4 7.4 %fusion.2 = f32[2]{0:T(128)S(1)} fusion(f32[2,256,256]{2,1,0:T(8,128)S(1)} %fusion.9, bf16[2,256,6144]{1,2,0:T(8,128)(2,1)} %all-gather.5.cloned.1.call-done), kind=kOutput, calls=%fused_computation.11 | convolution fusion | flops 1610874880 | bytes 6815752 | tf_op jit(solution)/shard_map/btd,bsd->bts/dot_general | solution.py:46
  301.8 0.0 slice-done
  301.8 0.0 slice-done.1
  301.8 0.0 copy-start
  301.8 2.7 fusion.3
  304.5 0.1 pad_maximum_fusion.1
  304.6 0.6 broadcast_in_dim.4
  305.2 10.8 %all-to-all-start = ((f32[64,1,4]{2,1,0:T(1,128)}), f32[64,1,4]{2,1,0:T(1,128)S(1)}, u32[]{:S(2)}, u32[]{:S(2)}) async-start(f32[64,1,4]{2,1,0:T(1,128)} %broadcast_in_dim.4), calls=%async_computation | async-start | bytes 65536 | tf_op jit(solution)/shard_map/all_to_all | solution.py:12
  316.1 0.2 reduce-scatter.2.cloned.1.call-start
  316.3 0.2 copy.34
  316.5 8.8 %all-to-all-done = f32[64,1,4]{2,1,0:T(1,128)S(1)} async-done(((f32[64,1,4]{2,1,0:T(1,128)}), f32[64,1,4]{2,1,0:T(1,128)S(1)}, u32[]{:S(2)}, u32[]{:S(2)}) %all-to-all-start) | async-done | bytes 1056 | tf_op jit(solution)/shard_map/all_to_all | solution.py:12
  325.3 0.1 reduce_sum.38
  325.4 0.1 sqrt_bitcast_fusion.1
  325.5 0.0 copy-done
  325.5 0.1 pad_maximum_fusion
  325.5 8.6 %fusion = bf16[6144,384]{0,1:T(8,128)(2,1)} fusion(bf16[2,256,6144]{1,2,0:T(8,128)(2,1)} %all-gather.5.cloned.1.call-done, bf16[2,256,384]{1,2,0:T(8,128)(2,1)S(1)} %copy.34, f32[2]{0:T(128)S(1)} %get-tuple-element.21), kind=kOutput, calls=%fused_computation.4 | convolution fusion | flops 2418868224 | bytes 11403272 | tf_op jit(solution)/shard_map/dot_general | solution.py:91
  334.2 0.0 reduce-scatter.2.cloned.1.call-update
  334.2 7.5 %multiply_convert_fusion = bf16[2,256,6144]{1,2,0:T(8,128)(2,1)} fusion(bf16[2,256,6144]{1,2,0:T(8,128)(2,1)} %all-gather.7.cloned.1.call-done, f32[2]{0:T(128)S(1)} %get-tuple-element.20), kind=kLoop, calls=%fused_computation | loop fusion | flops 9437184 | bytes 12582920 | tf_op jit(solution)/shard_map/convert_element_type | solution.py:86
  341.7 8.7 %copy.35 = bf16[2,256,6144]{2,1,0:T(8,128)(2,1)} copy(bf16[2,256,6144]{1,2,0:T(8,128)(2,1)} %multiply_convert_fusion) | data formatting | bytes 12582912 | tf_op jit(solution)/shard_map/convert_element_type | solution.py:86
  350.4 5.4 %convolution_convert_fusion = bf16[384,6144]{1,0:T(8,128)(2,1)S(1)} fusion(bf16[512,384]{1,0:T(8,128)(2,1)S(1)} %get-tuple-element.24, bf16[512,6144]{1,0:T(8,128)(2,1)} %bitcast.43), kind=kOutput, calls=%fused_computation.3 | convolution fusion | flops 2418278400 | bytes 11403264 | tf_op jit(solution)/shard_map/dot_general | solution.py:98
  355.8 2.6 copy.44
  358.4 4.9 %all-to-all-start.1 = ((bf16[4,384,1536]{2,1,0:T(8,128)(2,1)}), bf16[4,384,1536]{2,1,0:T(8,128)(2,1)}, u32[]{:S(2)}, u32[]{:S(2)}) async-start(bf16[4,384,1536]{2,1,0:T(8,128)(2,1)} %bitcast.44), calls=%async_computation.2 | async-start | bytes 9437184 | tf_op jit(solution)/shard_map/all_to_all | solution.py:36
  363.3 0.6 copy.38
  364.0 67.2 %all-to-all-done.1 = bf16[4,384,1536]{2,1,0:T(8,128)(2,1)} async-done(((bf16[4,384,1536]{2,1,0:T(8,128)(2,1)}), bf16[4,384,1536]{2,1,0:T(8,128)(2,1)}, u32[]{:S(2)}, u32[]{:S(2)}) %all-to-all-start.1) | async-done | bytes 4718624 | tf_op jit(solution)/shard_map/all_to_all | solution.py:36
  431.2 4.7 %convert_reduce_fusion = f32[384,1536]{1,0:T(8,128)} fusion(bf16[4,384,1536]{2,1,0:T(8,128)(2,1)} %all-to-all-done.1), kind=kLoop, calls=%fused_computation.2 | loop fusion | flops 4128768 | bytes 7077888 | tf_op jit(solution)/shard_map/reduce_sum | solution.py:37
  435.9 0.0 reduce-scatter.2.cloned.1.call-done
  435.9 2.7 copy.37
  (2 shorter events, 0.0 us)
Async XLA Ops:
  7.2 88.4 %all-gather.5.cloned.1.call-start = ((), (), s32[]{:S(2)}) async-start(), calls=%async_computation.3 | async-start | bytes 6389760 | tf_op jit(solution)/shard_map/all_gather | solution.py:52
  7.9 167.7 %all-gather.7.cloned.1.call-start = ((), (), s32[]{:S(2)}) async-start(), calls=%async_computation.4 | async-start | bytes 6389760 | tf_op jit(solution)/shard_map/all_gather | solution.py:59
  8.6 220.1 %all-gather.11.cloned.1.call-start = ((), (), s32[]{:S(2)}) async-start(), calls=%async_computation.6 | async-start | bytes 5898240 | tf_op jit(solution)/shard_map/all_gather | solution.py:56
  9.4 276.6 %all-gather.9.cloned.1.call-start = ((), (), s32[]{:S(2)}) async-start(), calls=%async_computation.5 | async-start | bytes 5898240 | tf_op jit(solution)/shard_map/all_gather | solution.py:63
  294.0 7.8 %slice-start = ((s8[6291456]{0:T(1024)(128)(4,1)}), s8[4194304]{0:T(1024)(128)(4,1)S(1)}, s32[]{:S(2)}) async-start(s8[6291456]{0:T(1024)(128)(4,1)} %bitcast.41), calls=%async_computation.8 | async-start | bytes 8388608
  294.4 7.4 %slice-start.1 = ((s8[6291456]{0:T(1024)(128)(4,1)}), s8[2097152]{0:T(1024)(128)(4,1)S(1)}, s32[]{:S(2)}) async-start(s8[6291456]{0:T(1024)(128)(4,1)} %bitcast.41), calls=%async_computation.9 | async-start | bytes 4194304
  301.8 23.7 %copy-start = (f32[2]{0:T(128)S(1)}, f32[2]{0:T(128)}, u32[]{:S(2)}) copy-start(f32[2]{0:T(128)} %param.9) | copy-start | bytes 28
  305.2 20.1 %all-to-all-start = ((f32[64,1,4]{2,1,0:T(1,128)}), f32[64,1,4]{2,1,0:T(1,128)S(1)}, u32[]{:S(2)}, u32[]{:S(2)}) async-start(f32[64,1,4]{2,1,0:T(1,128)} %broadcast_in_dim.4), calls=%async_computation | async-start | bytes 65536 | tf_op jit(solution)/shard_map/all_to_all | solution.py:12
  316.1 119.8 %reduce-scatter.2.cloned.1.call-start = ((), (), s32[]{:S(2)}) async-start(), calls=%async_computation.7 | async-start | bytes 5898240 | tf_op jit(solution)/shard_map/reduce_scatter | solution.py:90
  358.4 72.8 %all-to-all-start.1 = ((bf16[4,384,1536]{2,1,0:T(8,128)(2,1)}), bf16[4,384,1536]{2,1,0:T(8,128)(2,1)}, u32[]{:S(2)}, u32[]{:S(2)}) async-start(bf16[4,384,1536]{2,1,0:T(8,128)(2,1)} %bitcast.44), calls=%async_computation.2 | async-start | bytes 9437184 | tf_op jit(solution)/shard_map/all_to_all | solution.py:36
Sparse Core Ops, SparseCore 0:
  10.8 84.6 all-gather.4
  98.3 77.2 all-gather.6
  177.4 51.2 all-gather.10
  230.4 55.5 all-gather.8
  334.3 59.8 reduce-scatter.1
where the time goes:
time: 446 us; the launch traced here: 445 us
  waiting for transfers between devices  330 us (74%)
  matrix products  39.5 us (9%)
  local copies, waits for them, and re-layouts  32.9 us (7%)
  starting transfers between devices  16.1 us (4%)
  between operations  13.9 us (3%)
  other arithmetic  12.4 us (3%)
    all_gather x1, waiting for transfers between devices, on_device(): lax.all_gather(inputs, 'mp', axis=2, tiled=True).reshape(count_rows, -1)  85.6 us
    all_gather x1, waiting for transfers between devices, on_device(): lax.all_gather(cotangent, 'mp', axis=2, tiled=True).reshape(count_rows, -1)  71.4 us
    all_to_all x1, waiting for transfers between devices, sum_at_owner(): lax.all_to_all(pieces, axis, split_axis=0, concat_axis=0, tiled=True)  67.2 us
    all_gather x1, waiting for transfers between devices, on_device(): lax.all_gather(w_down, 'dp', axis=1, tiled=True)  50.3 us
    all_gather x1, waiting for transfers between devices, on_device(): lax.all_gather(w_up, 'dp', axis=0, tiled=True)  44.5 us
    all_to_all x1, starting transfers between devices, sent_to_all(): return lax.all_to_all(copies, axis, split_axis=0, concat_axis=0, tiled=True)  10.8 us
    dot_general x4, matrix products, gram_of(): jnp.einsum('btd,bsd->bts', cube, cube, preferred_element_type=jnp.float32)  10.8 us
  transfers between devices with their start and end apart: 7, of which 6 were waited for; matrix products, arithmetic and copies ran while one was open for 12% of the time, Pallas kernels for 0%

commit v1 on v0

--- a/solution.py
+++ b/solution.py
@@ -5,6 +5,11 @@
 
 inv_root_two = 0.7071067811865476
 inv_root_two_pi = 0.3989422804014327
+
+
+def gather_from_all(value, axis, dim):
+    copies = jnp.concatenate([value] * lax.axis_size(axis), axis=dim)
+    return lax.all_to_all(copies, axis, dim, dim, tiled=True)
 
 
 def sent_to_all(shard, axis):
@@ -49,7 +54,7 @@
 def on_device(inputs, cotangent, w_up, w_down, thresholds):
     images, patches, local_feats = inputs.shape
     count_rows = images * patches
-    x_whole = lax.all_gather(inputs, "mp", axis=2, tiled=True).reshape(count_rows, -1)
+    x_whole = gather_from_all(inputs, "mp", 2).reshape(count_rows, -1)
     hidden_local = w_up.shape[1]
     columns = x_whole
     pre = jnp.dot(

time: 446 us -> 419 us (0.939)
  waiting for transfers between devices: 330 us -> 209 us
  local copies, waits for them, and re-layouts: 32.9 us -> 103 us
  blocking collectives: 0 us -> 14.9 us
    all_to_all x1, waiting for transfers between devices: 8.83 us -> 139 us  [gather_from_all(): return lax.all_to_all(copies, axis, dim, dim, tiled=True)]
    all_gather x1 -> x0, waiting for transfers between devices: 85.6 us -> none  [on_device(): lax.all_gather(inputs, 'mp', axis=2, tiled=True).reshape(count_rows, -1)]
    unnamed x8 -> x75, local copies, waits for them, and re-layouts: 3.37 us -> 82.3 us
    all_gather x1, waiting for transfers between devices: 71.4 us -> 0.01 us  [on_device(): lax.all_gather(cotangent, 'mp', axis=2, tiled=True).reshape(count_rows, -1)]
    all_gather x1, waiting for transfers between devices: 50.3 us -> 0.01 us  [on_device(): lax.all_gather(w_down, 'dp', axis=1, tiled=True)]
    all_gather x1, waiting for transfers between devices: 44.5 us -> 0.01 us  [on_device(): lax.all_gather(w_up, 'dp', axis=0, tiled=True)]
    all_to_all x0 -> x1, blocking collectives: none -> 14.9 us  [sent_to_all(): return lax.all_to_all(copies, axis, split_axis=0, concat_axis=0, tiled=True)]
    all_gather x1 -> x0, local copies, waits for them, and re-layouts: 8.67 us -> none  [on_device(): lax.all_gather(inputs, 'mp', axis=2, tiled=True).reshape(count_rows, -1)]
  transfers between devices with their start and end apart: 7 -> 6, of which waited for: 6 -> 2; matrix products, arithmetic and copies ran while one was open for 12% -> 33% of each run, Pallas kernels for 0% -> 0%
where the time goes in v1:
time: 419 us; the launch traced here: 417 us
  waiting for transfers between devices  209 us (50%)
  local copies, waits for them, and re-layouts  103 us (25%)
  matrix products  42 us (10%)
  starting transfers between devices  18.5 us (4%)
  other arithmetic  15.3 us (4%)
  blocking collectives  14.9 us (4%)
  between operations  13.9 us (3%)
    all_to_all x1, waiting for transfers between devices, gather_from_all(): return lax.all_to_all(copies, axis, dim, dim, tiled=True)  139 us
    unnamed x75, local copies, waits for them, and re-layouts  82.3 us
    all_to_all x1, waiting for transfers between devices, sum_at_owner(): lax.all_to_all(pieces, axis, split_axis=0, concat_axis=0, tiled=True)  68.1 us
    all_to_all x1, blocking collectives, sent_to_all(): return lax.all_to_all(copies, axis, split_axis=0, concat_axis=0, tiled=True)  14.9 us
    all_to_all x1, starting transfers between devices, gather_from_all(): return lax.all_to_all(copies, axis, dim, dim, tiled=True)  13.1 us
    dot_general x4, matrix products, gram_of(): jnp.einsum('btd,bsd->bts', cube, cube, preferred_element_type=jnp.float32)  11.6 us
    all_gather x1, local copies, waits for them, and re-layouts, on_device(): lax.all_gather(cotangent, 'mp', axis=2, tiled=True).reshape(count_rows, -1)  8.74 us
    convert_element_type x1, local copies, waits for them, and re-layouts, on_device(): cot_clip = (factor[:, 1][:, None, None] * dy_whole.reshape(images, patche...  8.72 us
  transfers between devices with their start and end apart: 6, of which 2 were waited for; matrix products, arithmetic and copies ran while one was open for 33% of the time, Pallas kernels for 0%

profile of v1, /device:TPU:1, one launch (start us, length us, event | category | flops | bytes accessed | tf_op | source)
XLA Modules:
  0.0 417.0 jit_solution(13515267550333373807)
XLA Ops:
  7.9 1.6 constant_dynamic-update-slice_fusion.63
  9.6 1.6 constant_dynamic-update-slice_fusion.62
  11.2 1.6 constant_dynamic-update-slice_fusion.61
  12.8 1.6 constant_dynamic-update-slice_fusion.60
  14.5 1.6 constant_dynamic-update-slice_fusion.59
  16.1 1.6 constant_dynamic-update-slice_fusion.58
  17.7 1.6 constant_dynamic-update-slice_fusion.57
  19.4 1.6 constant_dynamic-update-slice_fusion.56
  21.0 1.6 constant_dynamic-update-slice_fusion.55
  22.6 1.6 constant_dynamic-update-slice_fusion.54
  24.3 1.6 constant_dynamic-update-slice_fusion.53
  25.9 1.6 constant_dynamic-update-slice_fusion.52
  27.5 1.6 constant_dynamic-update-slice_fusion.51
  29.2 1.6 constant_dynamic-update-slice_fusion.50
  30.8 1.6 constant_dynamic-update-slice_fusion.49
  32.4 1.6 constant_dynamic-update-slice_fusion.48
  34.1 1.6 constant_dynamic-update-slice_fusion.47
  35.7 1.6 constant_dynamic-update-slice_fusion.46
  37.3 1.6 constant_dynamic-update-slice_fusion.45
  40.6 1.6 constant_dynamic-update-slice_fusion.43
  42.2 1.6 constant_dynamic-update-slice_fusion.42
  43.9 1.6 constant_dynamic-update-slice_fusion.41
  45.5 1.6 constant_dynamic-update-slice_fusion.40
  47.1 1.6 constant_dynamic-update-slice_fusion.39
  48.8 1.6 constant_dynamic-update-slice_fusion.38
  50.4 1.6 constant_dynamic-update-slice_fusion.37
  52.0 1.6 constant_dynamic-update-slice_fusion.36
  53.7 1.6 constant_dynamic-update-slice_fusion.35
  55.3 1.6 constant_dynamic-update-slice_fusion.34
  58.6 1.6 constant_dynamic-update-slice_fusion.32
  83.9 13.1 %all-to-all-start = ((bf16[2,256,6144]{1,0,2:T(2,128)(2,1)}), bf16[2,256,6144]{1,0,2:T(2,128)(2,1)}, u32[]{:S(2)}, u32[]{:S(2)}) async-start(bf16[2,256,6144]{1,0,2:T(2,128)(2,1)} %constant_dynamic-update-slice_fusion), calls=%async_computation | async-start | bytes 12582912 | tf_op jit(solution)/shard_map/all_to_all | solution.py:12
  98.8 139.1 %all-to-all-done = bf16[2,256,6144]{1,0,2:T(2,128)(2,1)} async-done(((bf16[2,256,6144]{1,0,2:T(2,128)(2,1)}), bf16[2,256,6144]{1,0,2:T(2,128)(2,1)}, u32[]{:S(2)}, u32[]{:S(2)}) %all-to-all-start) | async-done | bytes 6291488 | tf_op jit(solution)/shard_map/all_to_all | solution.py:12
  237.9 6.4 %copy.360 = bf16[768,8,2,256]{3,1,2,0:T(8,128)(2,1)} copy(bf16[768,8,2,256]{3,2,1,0:T(2,128)(2,1)} %bitcast.13) | data formatting | bytes 12582912
  244.3 8.7 %copy.350 = bf16[2,256,6144]{2,1,0:T(8,128)(2,1)} copy(bf16[2,256,6144]{1,2,0:T(8,128)(2,1)} %all-gather.4.cloned.1.call-done) | data formatting | bytes 12582912 | tf_op jit(solution)/shard_map/all_gather | solution.py:64
  253.1 8.5 %multiply_convert_fusion.2 = (bf16[512,384]{1,0:T(8,128)(2,1)S(1)}, f32[512,384]{1,0:T(8,128)}) fusion(bf16[512,6144]{0,1:T(8,128)(2,1)} %bitcast.39, bf16[6144,384]{1,0:T(8,128)(2,1)} %all-gather.8.cloned.1.call-done), kind=kOutput, calls=%fused_computation.20 | convolution fusion | flops 2416902144 | bytes 12189696 | tf_op jit(solution)/shard_map/dot_general | solution.py:60
  261.9 8.3 %fusion = f32[2,256,256]{2,1,0:T(8,128)} fusion(bf16[2,256,6144]{1,0,2:T(2,128)(2,1)} %all-to-all-done), kind=kOutput, calls=%fused_computation.4 | convolution fusion | flops 1610612736 | bytes 6815744 | tf_op jit(solution)/shard_map/btd,bsd->bts/dot_general | solution.py:51
  270.1 8.0 %fusion.3 = bf16[512,384]{1,0:T(8,128)(2,1)S(1)} fusion(bf16[512,6144]{1,0:T(8,128)(2,1)} %bitcast.43, bf16[384,6144]{1,0:T(8,128)(2,1)} %all-gather.6.cloned.1.call-done, f32[512,384]{1,0:T(8,128)} %get-tuple-element.25), kind=kOutput, calls=%fused_computation.9 | convolution fusion | flops 2417885184 | bytes 12189696 | tf_op jit(solution)/shard_map/dot_general | solution.py:66
  278.6 2.6 fusion.5
  281.3 14.9 %all_to_all.16 = f32[64,1,4]{2,1,0:T(1,128)S(1)} all-to-all(f32[64,1,4]{2,1,0:T(1,128)S(1)} %broadcast_in_dim.4), channel_id=1, replica_groups=mesh['dp'=4,'mp'=64] {'mp'}, dimensions={0} | all-to-all | bytes 2048 | tf_op jit(solution)/shard_map/all_to_all | solution.py:17
  296.5 8.4 %bitcast_convert_fusion = bf16[6144,384]{1,0:T(8,128)(2,1)} fusion(bf16[2,256,6144]{1,0,2:T(2,128)(2,1)} %all-to-all-done, bf16[2,256,384]{2,1,0:T(8,128)(2,1)S(1)} %bitcast.46, f32[2]{0:T(128)S(1)} %get-tuple-element.21), kind=kOutput, calls=%fused_computation.1 | convolution fusion | flops 2418868224 | bytes 11403272 | tf_op jit(solution)/shard_map/dot_general | solution.py:96
  304.9 7.6 %multiply_convert_fusion = bf16[2,256,6144]{1,2,0:T(8,128)(2,1)} fusion(bf16[2,256,6144]{1,2,0:T(8,128)(2,1)} %all-gather.4.cloned.1.call-done, f32[2]{0:T(128)S(1)} %get-tuple-element.20), kind=kLoop, calls=%fused_computation | loop fusion | flops 9437184 | bytes 12582920 | tf_op jit(solution)/shard_map/convert_element_type | solution.py:91
  312.5 8.7 %copy.353 = bf16[2,256,6144]{2,1,0:T(8,128)(2,1)} copy(bf16[2,256,6144]{1,2,0:T(8,128)(2,1)} %multiply_convert_fusion) | data formatting | bytes 12582912 | tf_op jit(solution)/shard_map/convert_element_type | solution.py:91
  321.2 5.5 %convolution_convert_fusion = bf16[384,6144]{1,0:T(8,128)(2,1)S(1)} fusion(bf16[512,384]{1,0:T(8,128)(2,1)S(1)} %get-tuple-element.24, bf16[512,6144]{1,0:T(8,128)(2,1)} %bitcast.40), kind=kOutput, calls=%fused_computation.3 | convolution fusion | flops 2418278400 | bytes 11403264 | tf_op jit(solution)/shard_map/dot_general | solution.py:103
  326.7 2.5 copy.430
  329.3 5.0 %all-to-all-start.2 = ((bf16[4,384,1536]{2,1,0:T(8,128)(2,1)}), bf16[4,384,1536]{2,1,0:T(8,128)(2,1)}, u32[]{:S(2)}, u32[]{:S(2)}) async-start(bf16[4,384,1536]{2,1,0:T(8,128)(2,1)} %bitcast.41), calls=%async_computation.3 | async-start | bytes 9437184 | tf_op jit(solution)/shard_map/all_to_all | solution.py:41
  334.9 68.1 %all-to-all-done.2 = bf16[4,384,1536]{2,1,0:T(8,128)(2,1)} async-done(((bf16[4,384,1536]{2,1,0:T(8,128)(2,1)}), bf16[4,384,1536]{2,1,0:T(8,128)(2,1)}, u32[]{:S(2)}, u32[]{:S(2)}) %all-to-all-start.2) | async-done | bytes 4718624 | tf_op jit(solution)/shard_map/all_to_all | solution.py:41
  403.0 4.7 %convert_reduce_fusion = f32[384,1536]{1,0:T(8,128)} fusion(bf16[4,384,1536]{2,1,0:T(8,128)(2,1)} %all-to-all-done.2), kind=kLoop, calls=%fused_computation.2 | loop fusion | flops 4128768 | bytes 7077888 | tf_op jit(solution)/shard_map/reduce_sum | solution.py:42
  407.7 2.8 convert_element_type.35
  (66 shorter events, 31.1 us)
Async XLA Ops:
  7.2 53.1 %copy-start = (bf16[2,256,96]{1,2,0:T(8,128)(2,1)S(1)}, bf16[2,256,96]{1,2,0:T(8,128)(2,1)}, u32[]{:S(2)}) copy-start(bf16[2,256,96]{1,2,0:T(8,128)(2,1)} %param.5) | copy-start | bytes 294916
  7.2 237.1 %all-gather.4.cloned.1.call-start = ((), (), s32[]{:S(2)}) async-start(), calls=%async_computation.4 | async-start | bytes 6389760 | tf_op jit(solution)/shard_map/all_gather | solution.py:64
  83.9 154.0 %all-to-all-start = ((bf16[2,256,6144]{1,0,2:T(2,128)(2,1)}), bf16[2,256,6144]{1,0,2:T(2,128)(2,1)}, u32[]{:S(2)}, u32[]{:S(2)}) async-start(bf16[2,256,6144]{1,0,2:T(2,128)(2,1)} %constant_dynamic-update-slice_fusion), calls=%async_computation | async-start | bytes 12582912 | tf_op jit(solution)/shard_map/all_to_all | solution.py:12
  97.1 156.0 %all-gather.8.cloned.1.call-start = ((), (), s32[]{:S(2)}) async-start(), calls=%async_computation.6 | async-start | bytes 5898240 | tf_op jit(solution)/shard_map/all_gather | solution.py:61
  97.8 172.3 %all-gather.6.cloned.1.call-start = ((), (), s32[]{:S(2)}) async-start(), calls=%async_computation.5 | async-start | bytes 5898240 | tf_op jit(solution)/shard_map/all_gather | solution.py:68
  98.5 309.1 %reduce-scatter.2.cloned.1.call-start = ((), (), s32[]{:S(2)}) async-start(), calls=%async_computation.7 | async-start | bytes 5898240 | tf_op jit(solution)/shard_map/reduce_scatter | solution.py:95
  261.9 16.7 %slice-start = ((s8[6291456]{0:T(1024)(128)(4,1)}), s8[2097152]{0:T(1024)(128)(4,1)S(1)}, s32[]{:S(2)}) async-start(s8[6291456]{0:T(1024)(128)(4,1)} %bitcast.37), calls=%async_computation.8 | async-start | bytes 4194304
  270.1 8.0 %copy-start.1 = (f32[2,256,256]{2,1,0:T(8,128)S(1)}, f32[2,256,256]{2,1,0:T(8,128)}, u32[]{:S(2)}) copy-start(f32[2,256,256]{2,1,0:T(8,128)} %fusion) | copy-start | bytes 1572868
  270.1 8.5 %slice-start.1 = ((s8[6291456]{0:T(1024)(128)(4,1)}), s8[4194304]{0:T(1024)(128)(4,1)S(1)}, s32[]{:S(2)}) async-start(s8[6291456]{0:T(1024)(128)(4,1)} %bitcast.37), calls=%async_computation.9 | async-start | bytes 8388608
  278.6 17.8 %copy-start.2 = (f32[2]{0:T(128)S(1)}, f32[2]{0:T(128)}, u32[]{:S(2)}) copy-start(f32[2]{0:T(128)} %param.9) | copy-start | bytes 28
  329.3 73.7 %all-to-all-start.2 = ((bf16[4,384,1536]{2,1,0:T(8,128)(2,1)}), bf16[4,384,1536]{2,1,0:T(8,128)(2,1)}, u32[]{:S(2)}, u32[]{:S(2)}) async-start(bf16[4,384,1536]{2,1,0:T(8,128)(2,1)} %bitcast.41), calls=%async_computation.3 | async-start | bytes 9437184 | tf_op jit(solution)/shard_map/all_to_all | solution.py:41
Sparse Core Ops, SparseCore 0:
  10.8 84.6 all-gather.3
  99.7 56.0 all-gather.7
  157.6 55.5 all-gather.5
  305.0 61.6 reduce-scatter.1
